TPU v7x, 128 devices: a whole 4x4x4 slice. The times are simulated.
128 devices in a mesh: fsdp: 32 (over y, x_lo, z), tp: 4 (over x_hi, core).
Axes of the slice: x: 4 (x_hi: 2, x_lo: 2; x = x_hi * 2 + x_lo), y: 4, z: 4, core: 2. Of those that a mesh axis runs over, the one named last changes fastest.
Arguments:
- inputs: bfloat16 [8192, 1024], P('fsdp'), may hold values from -6 to 6
- out_grads: bfloat16 [8192, 24, 1024], P('fsdp', None, 'tp'), may hold values from -0.0625 to 0.0625
- momentum: float32 [1024, 24, 1024], P('fsdp', None, 'tp'), may hold values from -6 to 6
Outputs:
- new_momentum: float32 [1024, 24, 1024], P('fsdp', None, 'tp')
- update: float32 [1024, 24, 1024], P('fsdp', None, 'tp')
All inputs are finite; a program needn't handle non-finite values.
Results may differ from a plain program's by a relative error of at most 0.01.
Values may be sent and summed in bfloat16 or wider, within the bound.
A program may use at most 128 MiB of HBM per device.

v0:
```python
import math

import jax
import jax.numpy as jnp
from jax import lax
from jax.sharding import PartitionSpec as P

ITERS = 2


def iterate(current, summed):
    for turn in range(ITERS):
        partial_gram = jnp.einsum(
            "sic,sjc->sij", current, current, preferred_element_type=jnp.float32
        )
        gram = summed(partial_gram).astype(jnp.bfloat16)
        square = jnp.einsum("sij,sjk->sik", gram, gram, preferred_element_type=jnp.float32)
        mixer = (-4.775 * gram.astype(jnp.float32) + 2.0315 * square).astype(jnp.bfloat16)
        product = jnp.einsum("sij,sjc->sic", mixer, current, preferred_element_type=jnp.float32)
        current = (3.4445 * current.astype(jnp.float32) + product).astype(jnp.bfloat16)
    return current


def keep_local(value):
    return value


def local(inputs, out_grads, momentum):
    groups = lax.axis_size("fsdp")
    count = out_grads.shape[1]
    slots = (count + groups - 1) // groups
    width = inputs.shape[1]
    cols = out_grads.shape[2]
    rows_here = momentum.shape[0]
    matrix_ids = jnp.arange(count, dtype=jnp.int32)
    places = matrix_ids % groups * slots + matrix_ids // groups
    select = jnp.arange(groups * slots, dtype=jnp.int32)[:, None] == places[None, :]
    select_low = select.astype(jnp.bfloat16)
    grads = lax.psum_scatter(
        jnp.einsum("tx,tmc->xmc", inputs, out_grads, preferred_element_type=jnp.float32),
        "fsdp",
        scatter_dimension=0,
        tiled=True,
    )
    new_momentum = 0.95 * momentum + grads
    nesterov = (grads + 0.95 * new_momentum).astype(jnp.bfloat16)
    outgoing = jnp.einsum(
        "pm,rmc->prc", select_low, nesterov, preferred_element_type=jnp.float32
    ).astype(jnp.bfloat16)
    outgoing = outgoing.reshape(groups, slots, rows_here, cols)
    arrived = lax.all_to_all(outgoing, "fsdp", split_axis=0, concat_axis=0, tiled=True)
    owned = arrived.transpose(1, 0, 2, 3).reshape(slots, width, cols)
    full_matrix = lax.all_gather(owned, "tp", axis=2, tiled=True)
    widened = full_matrix.astype(jnp.float32)
    scales = jnp.sqrt(jnp.sum(widened * widened, axis=(1, 2))) + 1e-07
    current = (widened / scales[:, None, None]).astype(jnp.bfloat16)
    finished = iterate(current, keep_local)
    final = lax.dynamic_slice_in_dim(finished, lax.axis_index("tp") * cols, cols, 2)
    going_back = final.reshape(slots, groups, rows_here, cols).transpose(1, 0, 2, 3)
    returned = lax.all_to_all(going_back, "fsdp", split_axis=0, concat_axis=0, tiled=True)
    returned_flat = returned.reshape(groups * slots, rows_here, cols)
    update = jnp.einsum(
        "pm,prc->rmc", select_low, returned_flat, preferred_element_type=jnp.float32
    ) * (0.2 * math.sqrt(width))
    return (new_momentum, update)


def solution(mesh):
    in_specs = (P("fsdp", None), P("fsdp", None, "tp"), P("fsdp", None, "tp"))
    out_specs = (P("fsdp", None, "tp"), P("fsdp", None, "tp"))
    return jax.shard_map(local, mesh=mesh, in_specs=in_specs, out_specs=out_specs, check_vma=False)
```

profile of v0, /device:TPU:0, one launch (start us, length us, event | category | flops | bytes accessed | tf_op | source)
XLA Modules:
  0.0 410.6 jit_solution(14658713412255461043)
XLA Ops:
  7.2 0.0 copy-start
  7.2 0.0 reduce-scatter.2.cloned.1.call-start
  7.2 1.8 copy-done
  9.1 11.2 %fusion.3 = f32[1024,24,256]{2,0,1:T(8,128)} fusion(bf16[256,24,256]{2,1,0:T(8,128)(2,1)S(1)} %copy-done, bf16[256,1024]{1,0:T(8,128)(2,1)} %param.3), kind=kOutput, calls=%fused_computation.8 | convolution fusion | flops 3221225472 | bytes 28835840 | tf_op jit(solution)/shard_map/tx,tmc->xmc/dot_general | solution.py:40
  20.3 0.0 reduce-scatter.2.cloned.1.call-update
  20.3 0.0 all-gather.2.cloned.1.call-start
  20.3 280.1 %reduce-scatter.2.cloned.1.call-done = f32[32,24,256]{2,0,1:T(8,128)} async-done(((f32[1024,24,256]{2,0,1:T(8,128)}), f32[32,24,256]{2,0,1:T(8,128)}) %reduce-scatter.2.cloned.1.call-update) | async-done | bytes 786448 | tf_op jit(solution)/shard_map/reduce_scatter | solution.py:39
  300.4 2.6 add_convert_fusion.2
  303.1 0.5 fusion.14
  303.5 0.3 copy.21
  303.8 15.4 %all_to_all.10 = bf16[32,1,32,256]{3,2,1,0:T(8,128)(2,1)} all-to-all(bf16[32,1,32,256]{3,2,1,0:T(8,128)(2,1)S(1)} %copy.21), channel_id=1, replica_groups=mesh['fsdp'=32,'tp'=4] {'fsdp'}, dimensions={0} | all-to-all | bytes 1048576 | tf_op jit(solution)/shard_map/all_to_all | solution.py:51
  319.2 0.0 all-gather.2.cloned.1.call-update
  319.3 24.6 %all-gather.2.cloned.1.call-done = bf16[1,1024,1024]{2,1,0:T(8,128)(2,1)} async-done(((bf16[1,1024,256]{2,1,0:T(8,128)(2,1)}), bf16[1,1024,1024]{2,1,0:T(8,128)(2,1)}) %all-gather.2.cloned.1.call-update) | async-done | bytes 2097168 | tf_op jit(solution)/shard_map/all_gather | solution.py:53
  343.9 3.3 fusion
  347.9 5.9 %fusion.9 = bf16[1024,1024]{1,0:T(8,128)(2,1)} fusion(bf16[1,1024,1024]{2,1,0:T(8,128)(2,1)} %all-gather.2.cloned.1.call-done, f32[]{:T(128)S(6)} %add.59), kind=kOutput, calls=%fused_computation.15 | convolution fusion | flops 2150629376 | bytes 4194308 | tf_op jit(solution)/shard_map/sic,sjc->sij/dot_general | solution.py:13
  353.8 10.1 %fusion.2 = bf16[1,1024,1024]{2,1,0:T(8,128)(2,1)} fusion(bf16[1024,1024]{1,0:T(8,128)(2,1)} %fusion.9, f32[]{:T(128)S(6)} %add.59, bf16[1,1024,1024]{2,1,0:T(8,128)(2,1)} %all-gather.2.cloned.1.call-done), kind=kOutput, calls=%fused_computation.5 | convolution fusion | flops 4310695936 | bytes 6291460 | tf_op jit(solution)/shard_map/sij,sjc->sic/dot_general | solution.py:19
  363.8 5.9 %fusion.6 = bf16[1024,1024]{1,0:T(8,128)(2,1)} fusion(bf16[1,1024,1024]{2,1,0:T(8,128)(2,1)} %fusion.2), kind=kOutput, calls=%fused_computation.12 | convolution fusion | flops 2147483648 | bytes 4194304 | tf_op jit(solution)/shard_map/sic,sjc->sij/dot_general | solution.py:13
  369.8 10.1 %convolution_bitcast_fusion = f32[1,1024,1024]{2,1,0:T(8,128)} fusion(bf16[1,1024,1024]{2,1,0:T(8,128)(2,1)} %fusion.2, bf16[1024,1024]{1,0:T(8,128)(2,1)} %fusion.6), kind=kOutput, calls=%fused_computation.10 | convolution fusion | flops 4300210176 | bytes 8388608 | tf_op jit(solution)/shard_map/sij,sjc->sic/dot_general | solution.py:19
  379.9 2.3 fusion.15
  382.2 7.4 %all-to-all-start.1 = ((bf16[32,1,32,256]{3,2,1,0:T(8,128)(2,1)}), bf16[32,1,32,256]{3,2,1,0:T(8,128)(2,1)}, u32[]{:S(2)}, u32[]{:S(2)}) async-start(bf16[32,1,32,256]{3,2,1,0:T(8,128)(2,1)} %bitcast.38), calls=%async_computation.2 | async-start | bytes 1048576 | tf_op jit(solution)/shard_map/all_to_all | solution.py:60
  389.6 2.5 copy.24
  392.1 9.4 %all-to-all-done.1 = bf16[32,1,32,256]{3,2,1,0:T(8,128)(2,1)} async-done(((bf16[32,1,32,256]{3,2,1,0:T(8,128)(2,1)}), bf16[32,1,32,256]{3,2,1,0:T(8,128)(2,1)}, u32[]{:S(2)}, u32[]{:S(2)}) %all-to-all-start.1) | async-done | bytes 524320 | tf_op jit(solution)/shard_map/all_to_all | solution.py:60
  401.4 2.3 fusion.13
  (1 shorter events, 0.0 us)
Async XLA Ops:
  7.2 1.9 copy-start
  7.2 293.3 %reduce-scatter.2.cloned.1.call-start = ((), (), s32[]{:S(2)}) async-start(), calls=%async_computation.3 | async-start | bytes 25952256 | tf_op jit(solution)/shard_map/reduce_scatter | solution.py:39
  20.3 323.6 %all-gather.2.cloned.1.call-start = ((), (), s32[]{:S(2)}) async-start(), calls=%async_computation.4 | async-start | bytes 2621440 | tf_op jit(solution)/shard_map/all_gather | solution.py:53
  382.2 19.3 %all-to-all-start.1 = ((bf16[32,1,32,256]{3,2,1,0:T(8,128)(2,1)}), bf16[32,1,32,256]{3,2,1,0:T(8,128)(2,1)}, u32[]{:S(2)}, u32[]{:S(2)}) async-start(bf16[32,1,32,256]{3,2,1,0:T(8,128)(2,1)} %bitcast.38), calls=%async_computation.2 | async-start | bytes 1048576 | tf_op jit(solution)/shard_map/all_to_all | solution.py:60
Sparse Core Ops, SparseCore 0:
  20.4 279.9 reduce-scatter.1
  319.4 24.4 all-gather.1
where the time goes:
time: 411 us
  waiting for transfers between devices  314 us (76%)
  matrix products  46 us (11%)
  blocking collectives  15.4 us (4%)
  between operations  14.8 us (4%)
  other arithmetic  8.22 us (2%)
  starting transfers between devices  7.48 us (2%)
  local copies, waits for them, and re-layouts  4.61 us (1%)
    reduce_scatter x1, waiting for transfers between devices, local(): lax.psum_scatter(jnp.einsum('tx,tmc->xmc', inputs, out_grads, preferred_e...  280 us
    all_gather x1, waiting for transfers between devices, local(): full_matrix = lax.all_gather(owned, 'tp', axis=2, tiled=True)  24.6 us
    dot_general x2, matrix products, iterate(): jnp.einsum('sij,sjc->sic', mixer, current, preferred_element_type=jnp.flo...  20.2 us
    all_to_all x1, blocking collectives, local(): lax.all_to_all(outgoing, 'fsdp', split_axis=0, concat_axis=0, tiled=True)  15.4 us
    dot_general x2, matrix products, iterate(): jnp.einsum('sic,sjc->sij', current, current, preferred_element_type=jnp.f...  11.8 us
    dot_general x1, matrix products, local(): jnp.einsum('tx,tmc->xmc', inputs, out_grads, preferred_element_type=jnp.f...  11.2 us
    all_to_all x1, waiting for transfers between devices, local(): lax.all_to_all(going_back, 'fsdp', split_axis=0, concat_axis=0, tiled=True)  9.38 us
  transfers between devices with their start and end apart: 3, of which 3 were waited for; matrix products, arithmetic and copies ran while one was open for 1% of the time, Pallas kernels for 0%

commit v1 on v0

v1 whole, which is shorter than its diff:
```python
import functools
import math

import jax
import jax.numpy as jnp
from jax import lax
from jax.experimental import pallas as pl
from jax.experimental.pallas import tpu as pltpu
from jax.sharding import PartitionSpec as P

ITERS = 2
NZ = 4
MESH = pl.DeviceIdType.MESH
F32 = jnp.float32
BF16 = jnp.bfloat16


def landed(ref, sem):
    pltpu.make_async_copy(ref, ref, sem).wait()


def gather_kernel(
    planes, xt_ref, og_ref, mom_ref, home_ref, full_ref,
    xall, ogs, moms, part, sums, gbuf, nbuf, full, home,
    x_s, x_r, f_s, f_r, og_s, og_r, mo_s, mo_r, rs_s, rs_r, n_s, n_r, nf_s, nf_r, h_s, h_r, loc,
):
    fs = lax.axis_index("fsdp")
    t = lax.axis_index("tp")
    p, z = fs // NZ, fs % NZ
    xh, c = t // 2, t % 2
    partner = xh * 2 + (1 - c)
    each = ogs.shape[0]
    tok = og_ref.shape[1]
    cols = og_ref.shape[2]
    rows = xall.shape[0]
    half = rows // 2
    block = rows // planes
    piece = block // NZ

    barrier = pltpu.get_barrier_semaphore()

    def greet(f, tp):
        pl.semaphore_signal(barrier, inc=1, device_id=(f, tp), device_id_type=MESH)

    for d in range(1, NZ):
        greet(p * NZ + (z + d) % NZ, t)
    for d in range(1, planes):
        for other in range(2):
            greet((p + d) % planes * NZ + z, other * 2 + c)
    greet(fs, (1 - xh) * 2 + c)
    greet(fs, partner)
    pl.semaphore_wait(barrier, NZ - 1 + 2 * (planes - 1) + 2)

    def x_view(slot, side):
        return xall.at[pl.ds(pl.multiple_of(side * half, half), half), pl.ds(pl.multiple_of(slot * tok, tok), tok)]

    def x_copy(d):
        return pltpu.make_async_remote_copy(
            xt_ref.at[pl.ds(pl.multiple_of(c * half, half), half), :], x_view(z, c), x_s.at[d], x_r.at[z],
            device_id=(p * NZ + (z + d) % NZ, t), device_id_type=MESH)

    def x_forward(slot):
        return pltpu.make_async_remote_copy(
            x_view(slot, c), x_view(slot, c), f_s.at[slot], f_r.at[slot],
            device_id=(fs, partner), device_id_type=MESH)

    def og_view(slot, k):
        return ogs.at[k, pl.ds(pl.multiple_of(slot * tok, tok), tok), :]

    def og_copy(d, k):
        to = (z + d) % NZ
        return pltpu.make_async_remote_copy(
            og_ref.at[to * each + k], og_view(z, k), og_s.at[k, d], og_r.at[k, z],
            device_id=(p * NZ + to, t), device_id_type=MESH)

    def mom_copy(d):
        to = (z + d) % NZ
        return pltpu.make_async_remote_copy(
            mom_ref.at[pl.ds(to * each, each)], moms.at[z], mo_s.at[d], mo_r.at[z],
            device_id=(p * NZ + to, t), device_id_type=MESH)

    own_x = pltpu.make_async_copy(xt_ref, xall.at[:, pl.ds(pl.multiple_of(z * tok, tok), tok)], loc.at[0])
    own_og = pltpu.make_async_copy(
        og_ref.at[pl.ds(z * each, each)], ogs.at[:, pl.ds(pl.multiple_of(z * tok, tok), tok), :], loc.at[1])
    own_mom = pltpu.make_async_copy(mom_ref.at[pl.ds(z * each, each)], moms.at[z], loc.at[2])

    for d in (2, 1, 3):
        x_copy(d).start()

    @pl.loop(0, each)
    def _(k):
        for d in (2, 1, 3):
            og_copy(d, k).start()

    for d in (2, 1, 3):
        mom_copy(d).start()
    own_x.start()
    own_og.start()
    own_mom.start()

    for d in (1, 3, 2):
        slot = (z + d) % NZ
        landed(x_view(slot, c), x_r.at[slot])
        x_forward(slot).start()
    own_x.wait()
    own_og.wait()
    own_mom.wait()
    for d in (1, 3, 2):
        slot = (z + d) % NZ
        landed(x_view(slot, 1 - c), f_r.at[slot])

    def rs_copy(k, to):
        return pltpu.make_async_remote_copy(
            part.at[k, to], sums.at[k, p], rs_s.at[k, to], rs_r.at[k, p],
            device_id=(to * NZ + z, t), device_id_type=MESH)

    def full_view(at, col):
        return full.at[pl.ds(pl.multiple_of(at * block, block), block), pl.ds(pl.multiple_of(col * cols, cols), cols)]

    def n_copy(k, other):
        return pltpu.make_async_remote_copy(
            nbuf.at[k], full_view(p, t), n_s.at[k, other], n_r.at[p, xh],
            device_id=(k * NZ + z, other * 2 + c), device_id_type=MESH)

    def n_local(k):
        return pltpu.make_async_copy(nbuf.at[k], full_view(p, t), n_r.at[p, xh])

    def multiply(k):
        for d in range(1, NZ):
            slot = (z + d) % NZ
            landed(og_view(slot, k), og_r.at[k, slot])
        step = 2 * block
        for r in range(planes // 2):
            acc = jnp.dot(xall[r * step:(r + 1) * step, :], ogs[k], preferred_element_type=F32)
            part[k, 2 * r] = acc[:block].astype(BF16)
            part[k, 2 * r + 1] = acc[block:].astype(BF16)
            for to in (2 * r, 2 * r + 1):
                @pl.when(p != to)
                def _():
                    rs_copy(k, to).start()

    def combine(k):
        total = part[k, p].astype(F32)
        for d in range(1, planes):
            source = (p + d) % planes
            landed(sums.at[k, source], rs_r.at[k, source])
            total = total + sums[k, source].astype(F32)
        momentum = moms[:, k].reshape(block, cols).astype(F32)
        gbuf[k] = total.astype(BF16)
        nbuf[k] = (total + 0.95 * (0.95 * momentum + total)).astype(BF16)
        for other in range(2):
            mine = jnp.logical_and(k == p, xh == other)

            @pl.when(jnp.logical_not(mine))
            def _():
                n_copy(k, other).start()

            @pl.when(mine)
            def _():
                n_local(k).start()

    multiply(0)
    for d in (1, 2, 3):
        slot = (z + d) % NZ
        landed(moms.at[slot], mo_r.at[slot])

    @pl.loop(1, each)
    def _(k):
        multiply(k)
        combine(k - 1)

    combine(each - 1)

    def home_copy(d):
        to = (z + d) % NZ
        return pltpu.make_async_remote_copy(
            gbuf.at[:, pl.ds(pl.multiple_of(to * piece, piece), piece), :], home.at[pl.ds(z * each, each)],
            h_s.at[d], h_r.at[z], device_id=(p * NZ + to, t), device_id_type=MESH)

    for d in range(1, NZ):
        home_copy(d).start()
    own_home = pltpu.make_async_copy(
        gbuf.at[:, pl.ds(pl.multiple_of(z * piece, piece), piece), :], home.at[pl.ds(z * each, each)], loc.at[3])
    own_home.start()

    def n_forward(at, other):
        return pltpu.make_async_remote_copy(
            full_view(at, other * 2 + c), full_view(at, other * 2 + c), nf_s.at[at, other], nf_r.at[at, other],
            device_id=(fs, partner), device_id_type=MESH)

    @pl.when(p < each)
    def _():
        @pl.loop(0, planes)
        def _(at):
            for other in range(2):
                landed(full_view(at, other * 2 + c), n_r.at[at, other])
                n_forward(at, other).start()

        @pl.loop(0, planes)
        def _(at):
            for other in range(2):
                landed(full_view(at, other * 2 + 1 - c), nf_r.at[at, other])
                n_forward(at, other).wait_send()

    full_ref[...] = full[...]
    own_home.wait()
    for d in range(1, NZ):
        slot = (z + d) % NZ
        landed(home.at[pl.ds(slot * each, each)], h_r.at[slot])
    home_ref[...] = home[...]

    for d in range(1, NZ):
        x_copy(d).wait_send()
        x_forward((z + d) % NZ).wait_send()
        mom_copy(d).wait_send()
        home_copy(d).wait_send()

    @pl.loop(0, each)
    def _(k):
        for d in range(1, NZ):
            og_copy(d, k).wait_send()
        for d in range(1, planes):
            rs_copy(k, (p + d) % planes).wait_send()
        for other in range(2):
            @pl.when(jnp.logical_not(jnp.logical_and(k == p, xh == other)))
            def _():
                n_copy(k, other).wait_send()


def newton_kernel(x_ref, out_ref, xs, gram, mix):
    rows = x_ref.shape[0]
    cols = out_ref.shape[1]
    step = 256
    start = pl.multiple_of(lax.axis_index("tp") * cols, cols)
    acc = jnp.zeros((step, rows), F32)
    for r in range(0, rows, step):
        wide = x_ref[r:r + step, :].astype(F32)
        acc = acc + wide * wide
    scale = jnp.sqrt(jnp.sum(acc)) + 1e-07
    inverse = 1.0 / scale
    for r in range(0, rows, step):
        xs[0, r:r + step, :] = (x_ref[r:r + step, :].astype(F32) * inverse).astype(BF16)
    for turn in range(ITERS):
        x = xs.at[turn]

        @pl.loop(0, rows, step=step)
        def _(r):
            here = pl.ds(pl.multiple_of(r, step), step)
            gram[here, :] = lax.dot_general(
                x[here, :], x[...], (((1,), (1,)), ((), ())), preferred_element_type=F32).astype(BF16)

        @pl.loop(0, rows, step=step)
        def _(r):
            here = pl.ds(pl.multiple_of(r, step), step)
            square = jnp.dot(gram[here, :], gram[...], preferred_element_type=F32)
            mix[here, :] = (-4.775 * gram[here, :].astype(F32) + 2.0315 * square).astype(BF16)

        @pl.loop(0, rows, step=step)
        def _(r):
            here = pl.ds(pl.multiple_of(r, step), step)
            wanted = pl.ds(start, cols) if turn == ITERS - 1 else slice(None)
            product = jnp.dot(mix[here, :], x[:, wanted], preferred_element_type=F32)
            result = (3.4445 * x[here, wanted].astype(F32) + product).astype(BF16)
            if turn == ITERS - 1:
                out_ref[here, :] = result
            else:
                xs[turn + 1, here, :] = result


def return_kernel(planes, groups, each, final_ref, out_ref, back, send, recv, loc):
    fs = lax.axis_index("fsdp")
    t = lax.axis_index("tp")
    p, z = fs // NZ, fs % NZ
    piece = back.shape[1]
    barrier = pltpu.get_barrier_semaphore()

    @pl.loop(1, groups)
    def _(d):
        pl.semaphore_signal(barrier, inc=1, device_id=((fs + d) % groups, t), device_id_type=MESH)

    pl.semaphore_wait(barrier, groups - 1)
    matrix = z * each + p

    def copy(to):
        return pltpu.make_async_remote_copy(
            final_ref.at[pl.ds(pl.multiple_of(to * piece, piece), piece), :], back.at[matrix], send.at[to],
            recv.at[matrix], device_id=(to, t), device_id_type=MESH)

    own = pltpu.make_async_copy(
        final_ref.at[pl.ds(pl.multiple_of(fs * piece, piece), piece), :], back.at[matrix], loc)

    @pl.when(p < each)
    def _():
        @pl.loop(1, groups)
        def _(d):
            copy((fs + d) % groups).start()

        own.start()
        own.wait()

    @pl.loop(0, groups)
    def _(source):
        sp, sz = source // NZ, source % NZ

        @pl.when(jnp.logical_and(sp < each, source != fs))
        def _():
            landed(back.at[sz * each + sp], recv.at[sz * each + sp])

    out_ref[...] = back[...]

    @pl.when(p < each)
    def _():
        @pl.loop(1, groups)
        def _(d):
            copy((fs + d) % groups).wait_send()


def local(inputs, out_grads, momentum):
    groups = lax.axis_size("fsdp")
    planes = groups // NZ
    tok, count, cols = out_grads.shape
    rows = inputs.shape[1]
    piece = momentum.shape[0]
    each = count // NZ
    block = rows // planes
    dma = pltpu.SemaphoreType.DMA
    vmem = pl.BlockSpec(memory_space=pltpu.VMEM)
    hbm = pl.BlockSpec(memory_space=pl.ANY)

    xt = inputs.T
    og = out_grads.transpose(1, 0, 2)
    mom = momentum.transpose(1, 0, 2).astype(BF16)
    home, full = pl.pallas_call(
        functools.partial(gather_kernel, planes),
        out_shape=(jax.ShapeDtypeStruct((count, piece, cols), BF16), jax.ShapeDtypeStruct((rows, rows), BF16)),
        in_specs=[hbm, hbm, hbm],
        out_specs=(vmem, vmem),
        scratch_shapes=[
            pltpu.VMEM((rows, NZ * tok), BF16),
            pltpu.VMEM((each, NZ * tok, cols), BF16),
            pltpu.VMEM((NZ, each, piece, cols), BF16),
            pltpu.VMEM((each, planes, block, cols), BF16),
            pltpu.VMEM((each, planes, block, cols), BF16),
            pltpu.VMEM((each, block, cols), BF16),
            pltpu.VMEM((each, block, cols), BF16),
            pltpu.VMEM((rows, rows), BF16),
            pltpu.VMEM((count, piece, cols), BF16),
            dma((NZ,)), dma((NZ,)), dma((NZ,)), dma((NZ,)),
            dma((each, NZ)), dma((each, NZ)), dma((NZ,)), dma((NZ,)),
            dma((each, planes)), dma((each, planes)),
            dma((each, 2)), dma((planes, 2)), dma((planes, 2)), dma((planes, 2)),
            dma((NZ,)), dma((NZ,)), dma((4,)),
        ],
        compiler_params=pltpu.CompilerParams(
            collective_id=0, has_side_effects=True, vmem_limit_bytes=48 * 1024 * 1024),
        name="gather",
    )(xt, og, mom)
    final = pl.pallas_call(
        newton_kernel,
        out_shape=jax.ShapeDtypeStruct((rows, cols), BF16),
        in_specs=[vmem],
        out_specs=vmem,
        scratch_shapes=[
            pltpu.VMEM((ITERS, rows, rows), BF16),
            pltpu.VMEM((rows, rows), BF16),
            pltpu.VMEM((rows, rows), BF16),
        ],
        compiler_params=pltpu.CompilerParams(vmem_limit_bytes=48 * 1024 * 1024),
        name="newton",
    )(full)
    back = pl.pallas_call(
        functools.partial(return_kernel, planes, groups, each),
        out_shape=jax.ShapeDtypeStruct((count, piece, cols), BF16),
        in_specs=[vmem],
        out_specs=vmem,
        scratch_shapes=[
            pltpu.VMEM((count, piece, cols), BF16),
            dma((groups,)), dma((count,)), dma,
        ],
        compiler_params=pltpu.CompilerParams(collective_id=1, has_side_effects=True),
        name="give_back",
    )(final)
    new_momentum = 0.95 * momentum + home.transpose(1, 0, 2).astype(F32)
    update = back.transpose(1, 0, 2).astype(F32) * (0.2 * math.sqrt(rows))
    return (new_momentum, update)


def solution(mesh):
    in_specs = (P("fsdp", None), P("fsdp", None, "tp"), P("fsdp", None, "tp"))
    out_specs = (P("fsdp", None, "tp"), P("fsdp", None, "tp"))
    return jax.shard_map(local, mesh=mesh, in_specs=in_specs, out_specs=out_specs, check_vma=False)
```

time: 411 us -> 167 us (0.41)
  waiting for transfers between devices: 314 us -> 0 us
  Pallas kernels: 0 us -> 154 us
  matrix products: 46 us -> 0 us
  blocking collectives: 15.4 us -> 0 us
  between operations: 14.8 us -> 0.69 us
  starting transfers between devices: 7.48 us -> 0 us
  other arithmetic: 8.22 us -> 1.38 us
  local copies, waits for them, and re-layouts: 4.61 us -> 10.3 us
    reduce_scatter x1 -> x0, waiting for transfers between devices: 280 us -> none  [local(): lax.psum_scatter(jnp.einsum('tx,tmc->xmc', inputs, out_grads, preferred_e...]
    pallas_call x0 -> x3, Pallas kernels: none -> 154 us  [the longest x1 111 us: local(): pl.pallas_call(functools.partial(gather_kernel, planes), out_shape=(jax.S...]
    dot_general x7 -> x0, matrix products: 46 us -> none  [the longest x2 20.2 us: iterate(): jnp.einsum('sij,sjc->sic', mixer, current, preferred_element_type=jnp.flo...]
    all_gather x1 -> x0, waiting for transfers between devices: 24.6 us -> none  [local(): full_matrix = lax.all_gather(owned, 'tp', axis=2, tiled=True)]
    all_to_all x1 -> x0, blocking collectives: 15.4 us -> none  [local(): lax.all_to_all(outgoing, 'fsdp', split_axis=0, concat_axis=0, tiled=True)]
    all_to_all x1 -> x0, waiting for transfers between devices: 9.38 us -> none  [local(): lax.all_to_all(going_back, 'fsdp', split_axis=0, concat_axis=0, tiled=True)]
    all_to_all x1 -> x0, starting transfers between devices: 7.4 us -> none  [local(): lax.all_to_all(going_back, 'fsdp', split_axis=0, concat_axis=0, tiled=True)]
    unnamed x3 -> x9, local copies, waits for them, and re-layouts: 4.32 us -> 10.3 us
  transfers between devices with their start and end apart: 3 -> 0, of which waited for: 3 -> 0; matrix products, arithmetic and copies ran while one was open for 1% -> 0% of each run, Pallas kernels for 0% -> 0%
where the time goes in v1:
time: 167 us
  Pallas kernels  154 us (92%)
  local copies, waits for them, and re-layouts  10.3 us (6%)
    pallas_call x1, Pallas kernels, local(): pl.pallas_call(functools.partial(gather_kernel, planes), out_shape=(jax.S...  111 us
    pallas_call x1, Pallas kernels, local(): pl.pallas_call(functools.partial(return_kernel, planes, groups, each), ou...  25.4 us
    pallas_call x1, Pallas kernels, local(): pl.pallas_call(newton_kernel, out_shape=jax.ShapeDtypeStruct((rows, cols)...  17.3 us
    unnamed x9, local copies, waits for them, and re-layouts  10.3 us

profile of v1, /device:TPU:0, one launch (start us, length us, event | category | flops | bytes accessed | tf_op | source)
XLA Modules:
  0.0 166.5 jit_solution(7843915861308269656)
XLA Ops:
  0.6 1.4 copy.17
  2.0 1.2 copy.6
  3.2 4.3 %copy.16 = bf16[256,24,256]{2,0,1:T(8,128)(2,1)} copy(bf16[256,24,256]{2,1,0:T(8,128)(2,1)} %param.4) | data formatting | bytes 6291456 | tf_op args[1]
  7.5 0.0 copy-start.1
  7.5 111.4 %gather.1 = (bf16[24,32,256]{2,1,0:T(8,128)(2,1)S(1)}, bf16[1024,1024]{1,0:T(8,128)(2,1)S(1)}) custom-call(bf16[1024,256]{1,0:T(8,128)(2,1)S(1)} %bitcast.11, bf16[24,256,256]{2,1,0:T(8,128)(2,1)} %bitcast.13, bf16[24,32,256]{2,1,0:T(8,128)(2,1)S(1)} %bitcast.12), custom_call_target="tpu_custom_call" | custom-call | tf_op jit(solution)/shard_map/gather/pallas_call | solution.py:333
  118.9 0.0 copy-done.1
  119.0 0.3 bitcast_add_fusion
  119.3 1.3 copy.9
  120.6 17.3 %newton.1.final_ref = bf16[1024,256]{1,0:T(8,128)(2,1)S(1)} custom-call(bf16[1024,1024]{1,0:T(8,128)(2,1)S(1)} %get-tuple-element.5.x_ref), custom_call_target="tpu_custom_call" | custom-call | tf_op jit(solution)/shard_map/newton/pallas_call | solution.py:358
  137.9 0.0 copy-start
  137.9 0.8 copy-done
  138.7 25.4 %give_back.1 = bf16[24,32,256]{2,1,0:T(8,128)(2,1)} custom-call(bf16[1024,256]{1,0:T(8,128)(2,1)} %copy-done), custom_call_target="tpu_custom_call" | custom-call | tf_op jit(solution)/shard_map/give_back/pallas_call | solution.py:371
  164.1 1.1 multiply_bitcast_fusion
  165.2 1.3 copy.10
Async XLA Ops:
  7.5 111.4 %copy-start.1 = (f32[32,24,256]{2,1,0:T(8,128)S(1)}, f32[32,24,256]{2,1,0:T(8,128)}, u32[]{:S(2)}) copy-start(f32[32,24,256]{2,1,0:T(8,128)} %param.5) | copy-start | bytes 2359300
  137.9 0.8 copy-start

commit v2 on v1

v2 whole, which is shorter than its diff:
```python
import functools
import math

import jax
import jax.numpy as jnp
from jax import lax
from jax.experimental import pallas as pl
from jax.experimental.pallas import tpu as pltpu
from jax.sharding import PartitionSpec as P

ITERS = 2
NZ = 4
MESH = pl.DeviceIdType.MESH
F32 = jnp.float32
BF16 = jnp.bfloat16


def landed(ref, sem):
    pltpu.make_async_copy(ref, ref, sem).wait()


def step_kernel(
    groups, x_ref, grads_ref, momentum_ref, home, back,
    xt_ref, og_ref, mom_ref, xall, ogs, moms, part, sums, gbuf, nbuf, full, xs, gram, mix, final,
    x_s, x_r, f_s, f_r, og_s, og_r, mo_s, mo_r, rs_s, rs_r, n_s, n_r, nf_s, nf_r, h_s, h_r, b_s, b_r, loc,
):
    planes = groups // NZ
    fs = lax.axis_index("fsdp")
    t = lax.axis_index("tp")
    p, z = fs // NZ, fs % NZ
    xh, c = t // 2, t % 2
    partner = xh * 2 + (1 - c)
    each = ogs.shape[0]
    tok = og_ref.shape[1]
    cols = og_ref.shape[2]
    rows = xall.shape[0]
    half = rows // 2
    block = rows // planes
    piece = block // NZ
    pairs = each // 2
    lanes = cols // 2

    barrier = pltpu.get_barrier_semaphore()

    def greet(f, tp):
        pl.semaphore_signal(barrier, inc=1, device_id=(f, tp), device_id_type=MESH)

    @pl.loop(1, groups)
    def _(d):
        greet((fs + d) % groups, t)

    @pl.loop(0, planes)
    def _(at):
        greet(at * NZ + z, (1 - xh) * 2 + c)

    greet(fs, partner)
    xt_ref[...] = x_ref[...].T

    def places():
        for m in range(NZ * each):
            for h in range(2):
                low = m % each
                yield m, h, m - low + h * pairs + low // 2, low % 2 * lanes

    @pl.loop(0, tok, step=16)
    def _(at):
        here = pl.ds(pl.multiple_of(at, 16), 16)
        turned = jnp.swapaxes(grads_ref[here].astype(F32), 0, 1).astype(BF16)
        for m, h, to, lane in places():
            og_ref[to, here, lane:lane + lanes] = turned[m, :, h * lanes:(h + 1) * lanes]

    turned = jnp.swapaxes(momentum_ref[...], 0, 1).astype(BF16)
    for m, h, to, lane in places():
        mom_ref[to, :, lane:lane + lanes] = turned[m, :, h * lanes:(h + 1) * lanes]
    pl.semaphore_wait(barrier, groups + planes)

    def x_view(slot, side):
        return xall.at[pl.ds(pl.multiple_of(side * half, half), half), pl.ds(pl.multiple_of(slot * tok, tok), tok)]

    def x_copy(d):
        return pltpu.make_async_remote_copy(
            xt_ref.at[pl.ds(pl.multiple_of(c * half, half), half), :], x_view(z, c), x_s.at[d], x_r.at[z],
            device_id=(p * NZ + (z + d) % NZ, t), device_id_type=MESH)

    def x_forward(slot):
        return pltpu.make_async_remote_copy(
            x_view(slot, c), x_view(slot, c), f_s.at[slot], f_r.at[slot],
            device_id=(fs, partner), device_id_type=MESH)

    def og_view(slot, k):
        return ogs.at[k, pl.ds(pl.multiple_of(slot * tok, tok), tok), :]

    def og_copy(d, k):
        to = (z + d) % NZ
        return pltpu.make_async_remote_copy(
            og_ref.at[to * each + k], og_view(z, k), og_s.at[k, d], og_r.at[k, z],
            device_id=(p * NZ + to, t), device_id_type=MESH)

    def mom_copy(d, k):
        to = (z + d) % NZ
        return pltpu.make_async_remote_copy(
            mom_ref.at[to * each + k], moms.at[z, k], mo_s.at[k, d], mo_r.at[k, z],
            device_id=(p * NZ + to, t), device_id_type=MESH)

    own_x = pltpu.make_async_copy(xt_ref, xall.at[:, pl.ds(pl.multiple_of(z * tok, tok), tok)], loc.at[0])
    own_og = pltpu.make_async_copy(
        og_ref.at[pl.ds(z * each, each)], ogs.at[:, pl.ds(pl.multiple_of(z * tok, tok), tok), :], loc.at[1])
    own_mom = pltpu.make_async_copy(mom_ref.at[pl.ds(z * each, each)], moms.at[z], loc.at[2])

    for d in (2, 1, 3):
        x_copy(d).start()

    @pl.loop(0, each)
    def _(k):
        for d in (2, 1, 3):
            og_copy(d, k).start()
        for d in (2, 1, 3):
            mom_copy(d, k).start()

    own_x.start()
    own_og.start()
    own_mom.start()

    for d in (1, 3, 2):
        slot = (z + d) % NZ
        landed(x_view(slot, c), x_r.at[slot])
        x_forward(slot).start()
    own_x.wait()
    own_og.wait()
    own_mom.wait()
    for d in (1, 3, 2):
        slot = (z + d) % NZ
        landed(x_view(slot, 1 - c), f_r.at[slot])

    def rs_copy(k, to):
        return pltpu.make_async_remote_copy(
            part.at[k, to], sums.at[k, p], rs_s.at[k, to], rs_r.at[k, p],
            device_id=(to * NZ + z, t), device_id_type=MESH)

    def half_view(at, col, h):
        return full.at[
            pl.ds(pl.multiple_of(at * block, block), block), pl.ds(pl.multiple_of(col * cols + h * lanes, lanes), lanes)]

    def n_copy(k, mm, other):
        h, pair = k // pairs, k % pairs
        return pltpu.make_async_remote_copy(
            nbuf.at[k, :, mm * lanes:(mm + 1) * lanes], half_view(p, t, h), n_s.at[k, mm, other], n_r.at[h, p, xh],
            device_id=((pair * 2 + mm) * NZ + z, other * 2 + c), device_id_type=MESH)

    def n_local(k, mm):
        h = k // pairs
        return pltpu.make_async_copy(nbuf.at[k, :, mm * lanes:(mm + 1) * lanes], half_view(p, t, h), n_r.at[h, p, xh])

    def n_mine(k, mm, other):
        return jnp.logical_and(k % pairs * 2 + mm == p, xh == other)

    def multiply(k):
        for d in range(1, NZ):
            slot = (z + d) % NZ
            landed(og_view(slot, k), og_r.at[k, slot])
        step = 2 * block
        for r in range(planes // 2):
            acc = jnp.dot(xall[r * step:(r + 1) * step, :], ogs[k], preferred_element_type=F32)
            part[k, 2 * r] = acc[:block].astype(BF16)
            part[k, 2 * r + 1] = acc[block:].astype(BF16)
            for to in (2 * r, 2 * r + 1):
                @pl.when(p != to)
                def _():
                    rs_copy(k, to).start()

    def combine(k):
        total = part[k, p].astype(F32)
        for d in range(1, planes):
            source = (p + d) % planes
            landed(sums.at[k, source], rs_r.at[k, source])
            total = total + sums[k, source].astype(F32)
        for d in range(1, NZ):
            slot = (z + d) % NZ
            landed(moms.at[slot, k], mo_r.at[k, slot])
        momentum = moms[:, k].reshape(block, cols).astype(F32)
        gbuf[k] = total.astype(BF16)
        nbuf[k] = (total + 0.95 * (0.95 * momentum + total)).astype(BF16)
        for mm in range(2):
            for other in range(2):
                mine = n_mine(k, mm, other)

                @pl.when(jnp.logical_not(mine))
                def _():
                    n_copy(k, mm, other).start()

                @pl.when(mine)
                def _():
                    n_local(k, mm).start()

    multiply(0)
    @pl.loop(1, each)
    def _(k):
        multiply(k)
        combine(k - 1)

    combine(each - 1)

    def home_copy(d):
        to = (z + d) % NZ
        return pltpu.make_async_remote_copy(
            gbuf.at[:, pl.ds(pl.multiple_of(to * piece, piece), piece), :], home.at[pl.ds(z * each, each)],
            h_s.at[d], h_r.at[z], device_id=(p * NZ + to, t), device_id_type=MESH)

    for d in range(1, NZ):
        home_copy(d).start()
    own_home = pltpu.make_async_copy(
        gbuf.at[:, pl.ds(pl.multiple_of(z * piece, piece), piece), :], home.at[pl.ds(z * each, each)], loc.at[3])
    own_home.start()

    def n_forward(h, at, other):
        view = half_view(at, other * 2 + c, h)
        return pltpu.make_async_remote_copy(
            view, view, nf_s.at[h, at, other], nf_r.at[h, at, other],
            device_id=(fs, partner), device_id_type=MESH)

    matrix = z * each + p

    def back_copy(to):
        return pltpu.make_async_remote_copy(
            final.at[pl.ds(pl.multiple_of(to * piece, piece), piece), :], back.at[matrix], b_s.at[to],
            b_r.at[matrix], device_id=(to, t), device_id_type=MESH)

    def newton():
        step = 256
        homes = step // piece
        wanted = pl.ds(pl.multiple_of(t * cols, cols), cols)
        acc = jnp.zeros((step, rows), F32)
        for r in range(0, rows, step):
            wide = full[r:r + step, :].astype(F32)
            acc = acc + wide * wide
        scale = jnp.sqrt(jnp.sum(acc)) + 1e-07
        inverse = 1.0 / scale
        for r in range(0, rows, step):
            xs[0, r:r + step, :] = (full[r:r + step, :].astype(F32) * inverse).astype(BF16)
        for turn in range(ITERS):
            x = xs.at[turn]

            @pl.loop(0, rows, step=step)
            def _(r):
                here = pl.ds(pl.multiple_of(r, step), step)
                gram[here, :] = lax.dot_general(
                    x[here, :], x[...], (((1,), (1,)), ((), ())), preferred_element_type=F32).astype(BF16)

            @pl.loop(0, rows, step=step)
            def _(r):
                here = pl.ds(pl.multiple_of(r, step), step)
                square = jnp.dot(gram[here, :], gram[...], preferred_element_type=F32)
                mix[here, :] = (-4.775 * gram[here, :].astype(F32) + 2.0315 * square).astype(BF16)

            @pl.loop(0, rows // step)
            def _(i):
                if turn < ITERS - 1:
                    here = pl.ds(pl.multiple_of(i * step, step), step)
                    product = jnp.dot(mix[here, :], x[...], preferred_element_type=F32)
                    xs[turn + 1, here, :] = (3.4445 * x[here, :].astype(F32) + product).astype(BF16)
                else:
                    part_at = (i + p) % (rows // step)
                    here = pl.ds(pl.multiple_of(part_at * step, step), step)
                    product = jnp.dot(mix[here, :], x[:, wanted], preferred_element_type=F32)
                    final[here, :] = (3.4445 * x[here, wanted].astype(F32) + product).astype(BF16)

                    @pl.loop(0, homes)
                    def _(h):
                        to = part_at * homes + (h + z) % homes

                        @pl.when(to != fs)
                        def _():
                            back_copy(to).start()

        own = pltpu.make_async_copy(
            final.at[pl.ds(pl.multiple_of(fs * piece, piece), piece), :], back.at[matrix], b_r.at[matrix])
        own.start()

    @pl.when(p < each)
    def _():
        for h in range(2):
            @pl.loop(0, planes)
            def _(step):
                at = (p + step) % planes
                for other in range(2):
                    landed(half_view(at, other * 2 + c, h), n_r.at[h, at, other])
                    n_forward(h, at, other).start()

        for h in range(2):
            @pl.loop(0, planes)
            def _(step):
                at = (p + step) % planes
                for other in range(2):
                    landed(half_view(at, other * 2 + 1 - c, h), nf_r.at[h, at, other])
                    n_forward(h, at, other).wait_send()

        newton()

    own_home.wait()
    for d in range(1, NZ):
        slot = (z + d) % NZ
        landed(home.at[pl.ds(slot * each, each)], h_r.at[slot])

    @pl.loop(0, groups)
    def _(source):
        sp, sz = source // NZ, source % NZ

        @pl.when(sp < each)
        def _():
            landed(back.at[sz * each + sp], b_r.at[sz * each + sp])

    @pl.when(p < each)
    def _():
        @pl.loop(1, groups)
        def _(d):
            back_copy((fs + d) % groups).wait_send()

    for d in range(1, NZ):
        x_copy(d).wait_send()
        x_forward((z + d) % NZ).wait_send()
        home_copy(d).wait_send()

    @pl.loop(0, each)
    def _(k):
        for d in range(1, NZ):
            og_copy(d, k).wait_send()
            mom_copy(d, k).wait_send()
        for d in range(1, planes):
            rs_copy(k, (p + d) % planes).wait_send()
        for mm in range(2):
            for other in range(2):
                @pl.when(jnp.logical_not(n_mine(k, mm, other)))
                def _():
                    n_copy(k, mm, other).wait_send()


def finish_kernel(each, rows, home, back, momentum_ref, new_ref, update_ref):
    count, piece, cols = home.shape
    pairs = each // 2
    lanes = cols // 2

    def grad(m, h):
        low = m % each
        lane = low % 2 * lanes
        return home[m - low + h * pairs + low // 2, :, lane:lane + lanes]

    for base in range(0, count, 8):
        group = slice(base, base + 8)
        update_ref[:, group, :] = jnp.swapaxes(back[group].astype(F32), 0, 1) * (0.2 * math.sqrt(rows))
        for h in range(2):
            here = slice(h * lanes, (h + 1) * lanes)
            grads = jnp.stack([grad(m, h) for m in range(base, base + 8)]).astype(F32)
            new_ref[:, group, here] = 0.95 * momentum_ref[:, group, here] + jnp.swapaxes(grads, 0, 1)


def local(inputs, out_grads, momentum):
    groups = lax.axis_size("fsdp")
    planes = groups // NZ
    tok, count, cols = out_grads.shape
    rows = inputs.shape[1]
    piece = momentum.shape[0]
    each = count // NZ
    block = rows // planes
    dma = pltpu.SemaphoreType.DMA
    vmem = pl.BlockSpec(memory_space=pltpu.VMEM)
    hbm = pl.BlockSpec(memory_space=pl.ANY)

    small = jax.ShapeDtypeStruct((count, piece, cols), BF16)
    home, back = pl.pallas_call(
        functools.partial(step_kernel, groups),
        out_shape=(small, small),
        in_specs=[vmem, vmem, vmem],
        out_specs=(hbm, hbm),
        scratch_shapes=[
            pltpu.VMEM((rows, tok), BF16),
            pltpu.VMEM((count, tok, cols), BF16),
            pltpu.VMEM((count, piece, cols), BF16),
            pltpu.VMEM((rows, NZ * tok), BF16),
            pltpu.VMEM((each, NZ * tok, cols), BF16),
            pltpu.VMEM((NZ, each, piece, cols), BF16),
            pltpu.VMEM((each, planes, block, cols), BF16),
            pltpu.VMEM((each, planes, block, cols), BF16),
            pltpu.VMEM((each, block, cols), BF16),
            pltpu.VMEM((each, block, cols), BF16),
            pltpu.VMEM((rows, rows), BF16),
            pltpu.VMEM((ITERS, rows, rows), BF16),
            pltpu.VMEM((rows, rows), BF16),
            pltpu.VMEM((rows, rows), BF16),
            pltpu.VMEM((rows, cols), BF16),
            dma((NZ,)), dma((NZ,)), dma((NZ,)), dma((NZ,)),
            dma((each, NZ)), dma((each, NZ)), dma((each, NZ)), dma((each, NZ)),
            dma((each, planes)), dma((each, planes)),
            dma((each, 2, 2)), dma((2, planes, 2)), dma((2, planes, 2)), dma((2, planes, 2)),
            dma((NZ,)), dma((NZ,)), dma((groups,)), dma((count,)), dma((4,)),
        ],
        compiler_params=pltpu.CompilerParams(
            collective_id=0, has_side_effects=True, vmem_limit_bytes=56 * 1024 * 1024),
        name="muon_step",
    )(inputs, out_grads, momentum)
    return pl.pallas_call(
        functools.partial(finish_kernel, each, rows),
        out_shape=(jax.ShapeDtypeStruct(momentum.shape, F32), jax.ShapeDtypeStruct(momentum.shape, F32)),
        in_specs=[vmem, vmem, vmem],
        out_specs=(vmem, vmem),
        name="finish",
    )(home, back, momentum)


def solution(mesh):
    in_specs = (P("fsdp", None), P("fsdp", None, "tp"), P("fsdp", None, "tp"))
    out_specs = (P("fsdp", None, "tp"), P("fsdp", None, "tp"))
    return jax.shard_map(local, mesh=mesh, in_specs=in_specs, out_specs=out_specs, check_vma=False)
```

time: 167 us -> 125 us (0.75)
  Pallas kernels: 154 us -> 124 us
  local copies, waits for them, and re-layouts: 10.3 us -> 0 us
    pallas_call x3 -> x2, Pallas kernels: 154 us -> 124 us  [the longest x1 121 us: local(): pl.pallas_call(functools.partial(step_kernel, groups), out_shape=(small,...]
    unnamed x9 -> x0, local copies, waits for them, and re-layouts: 10.3 us -> none
where the time goes in v2:
time: 125 us
  Pallas kernels  124 us (99%)
    pallas_call x1, Pallas kernels, local(): pl.pallas_call(functools.partial(step_kernel, groups), out_shape=(small,...  121 us
    pallas_call x1, Pallas kernels, local(): pl.pallas_call(functools.partial(finish_kernel, each, rows), out_shape=(j...  2.83 us

profile of v2, /device:TPU:0, one launch (start us, length us, event | category | flops | bytes accessed | tf_op | source)
XLA Modules:
  0.0 124.5 jit_solution(15817856966805742186)
XLA Ops:
  0.6 121.1 %muon_step.1 = (bf16[24,32,256]{2,1,0:T(8,128)(2,1)}, bf16[24,32,256]{2,1,0:T(8,128)(2,1)}) custom-call(bf16[256,1024]{1,0:T(8,128)(2,1)} %x_ref.1, bf16[256,24,256]{2,1,0:T(8,128)(2,1)} %grads_ref.1, f32[32,24,256]{2,1,0:T(8,128)} %momentum_ref.3), custom_call_target="tpu_custom_call" | custom-call | tf_op jit(solution)/shard_map/muon_step/pallas_call | solution.py:369
  121.7 2.8 %finish.1 = (f32[32,24,256]{2,1,0:T(8,128)}, f32[32,24,256]{2,1,0:T(8,128)}) custom-call(bf16[24,32,256]{2,1,0:T(8,128)(2,1)} %get-tuple-element.4.home, bf16[24,32,256]{2,1,0:T(8,128)(2,1)} %get-tuple-element.5.back, f32[32,24,256]{2,1,0:T(8,128)} %momentum_ref.3), custom_call_target="tpu_custom_call" | custom-call | tf_op jit(solution)/shard_map/finish/pallas_call | solution.py:400

commit v3 on v2

v3 whole, which is shorter than its diff:
```python
import functools
import math

import jax
import jax.numpy as jnp
from jax import lax
from jax.experimental import pallas as pl
from jax.experimental.pallas import tpu as pltpu
from jax.sharding import PartitionSpec as P

NZ = 4
MESH = pl.DeviceIdType.MESH
F32 = jnp.float32
BF16 = jnp.bfloat16


def landed(ref, sem):
    pltpu.make_async_copy(ref, ref, sem).wait()


def step_kernel(
    groups, x_ref, grads_ref, momentum_ref, home, back,
    xt_ref, og_ref, mom_ref, grads_in, momentum_in, xall, ogs, moms, part, sums, mids, kept, gbuf, nbuf,
    full, wide, xs, gram, mix, thin, final, squares,
    x_s, x_r, f_s, f_r, og_s, og_r, mo_s, mo_r, rs_s, rs_r, n_s, n_r, nf_s, nf_r, h_s, h_r, b_s, b_r, loc,
):
    planes = groups // NZ
    fs = lax.axis_index("fsdp")
    t = lax.axis_index("tp")
    p, z = fs // NZ, fs % NZ
    y, xl = p // 2, p % 2
    ny = groups // NZ // 2
    xh, c = t // 2, t % 2
    partner = xh * 2 + (1 - c)
    tok, count, cols = grads_ref.shape
    chunks = ogs.shape[0]
    each = chunks // 2
    rows = xall.shape[0]
    half = rows // 2
    block = rows // planes
    piece = block // NZ
    lanes = cols // 2

    load_grads = pltpu.make_async_copy(grads_ref, grads_in, loc.at[4])
    load_grads.start()
    load_momentum = pltpu.make_async_copy(momentum_ref, momentum_in, loc.at[5])
    load_momentum.start()

    barrier = pltpu.get_barrier_semaphore()

    def greet(f, tp):
        pl.semaphore_signal(barrier, inc=1, device_id=(f, tp), device_id_type=MESH)

    @pl.loop(1, groups)
    def _(d):
        greet((fs + d) % groups, t)

    @pl.loop(0, planes)
    def _(at):
        greet(at * NZ + z, (1 - xh) * 2 + c)

    greet(fs, partner)

    def x_view(slot, side):
        return xall.at[pl.ds(pl.multiple_of(side * half, half), half), pl.ds(pl.multiple_of(slot * tok, tok), tok)]

    def x_copy(d):
        return pltpu.make_async_remote_copy(
            xt_ref.at[pl.ds(pl.multiple_of(c * half, half), half), :], x_view(z, c), x_s.at[d], x_r.at[z],
            device_id=(p * NZ + (z + d) % NZ, t), device_id_type=MESH)

    def x_forward(slot):
        return pltpu.make_async_remote_copy(
            x_view(slot, c), x_view(slot, c), f_s.at[slot], f_r.at[slot],
            device_id=(fs, partner), device_id_type=MESH)

    def og_view(slot, k):
        return ogs.at[k, pl.ds(pl.multiple_of(slot * tok, tok), tok), :]

    def og_copy(d, k):
        to = (z + d) % NZ
        return pltpu.make_async_remote_copy(
            og_ref.at[to * chunks + k], og_view(z, k), og_s.at[k, d], og_r.at[k, z],
            device_id=(p * NZ + to, t), device_id_type=MESH)

    def mom_copy(d, h):
        to = (z + d) % NZ
        return pltpu.make_async_remote_copy(
            mom_ref.at[pl.ds(to * chunks + h * each, each)], moms.at[z, pl.ds(h * each, each)], mo_s.at[h, d],
            mo_r.at[h, z], device_id=(p * NZ + to, t), device_id_type=MESH)

    def places():
        for m in range(count):
            for h in range(2):
                yield m, h, m // each * chunks + h * each + m % each

    xt_ref[...] = x_ref[...].T
    pl.semaphore_wait(barrier, groups + planes)
    for d in (2, 1, 3):
        x_copy(d).start()

    load_grads.wait()

    @pl.loop(0, tok, step=16)
    def _(at):
        here = pl.ds(pl.multiple_of(at, 16), 16)
        turned = jnp.swapaxes(grads_in[here].astype(F32), 0, 1).astype(BF16)
        for m, h, to in places():
            og_ref[to, here, :] = turned[m, :, h * lanes:(h + 1) * lanes]

    def send_grads(low, high):
        @pl.loop(low, high)
        def _(k):
            for d in (2, 1, 3):
                og_copy(d, k).start()

    send_grads(0, 2)
    load_momentum.wait()
    turned = jnp.swapaxes(momentum_in[...], 0, 1).astype(BF16)
    for m, h, to in places():
        mom_ref[to] = turned[m, :, h * lanes:(h + 1) * lanes]
    for d in (2, 1, 3):
        mom_copy(d, 0).start()
    send_grads(2, chunks)
    for d in (2, 1, 3):
        mom_copy(d, 1).start()

    own_x = pltpu.make_async_copy(xt_ref, xall.at[:, pl.ds(pl.multiple_of(z * tok, tok), tok)], loc.at[0])
    own_og = pltpu.make_async_copy(
        og_ref.at[pl.ds(z * chunks, chunks)], ogs.at[:, pl.ds(pl.multiple_of(z * tok, tok), tok), :], loc.at[1])
    own_mom = pltpu.make_async_copy(mom_ref.at[pl.ds(z * chunks, chunks)], moms.at[z], loc.at[2])
    own_x.start()
    own_og.start()
    own_mom.start()

    for d in (1, 3, 2):
        slot = (z + d) % NZ
        landed(x_view(slot, c), x_r.at[slot])
        x_forward(slot).start()
    own_x.wait()
    own_og.wait()
    own_mom.wait()
    for d in (1, 3, 2):
        slot = (z + d) % NZ
        landed(x_view(slot, 1 - c), f_r.at[slot])

    def across_x(k, source, target):
        return pltpu.make_async_remote_copy(
            source, target, rs_s.at[k, 0], rs_r.at[k, ny],
            device_id=((y * 2 + 1 - xl) * NZ + z, t), device_id_type=MESH)

    def across_y(k, d, source, target):
        return pltpu.make_async_remote_copy(
            source, target, rs_s.at[k, d], rs_r.at[k, y],
            device_id=(((y + d) % ny * 2 + xl) * NZ + z, t), device_id_type=MESH)

    def x_then_y_first(k):
        return across_x(k, part.at[k, 1 - xl], sums.at[k, pl.ds(0, ny)])

    def x_then_y_second(k, d):
        return across_y(k, d, mids.at[k, (y + d) % ny], sums.at[k, ny + y])

    def y_then_x_first(k, d):
        return across_y(k, d, part.at[k, :, (y + d) % ny], sums.at[k, pl.ds(2 * y, 2)])

    def y_then_x_second(k):
        return across_x(k, mids.at[k, 0], sums.at[k, 2 * y])

    def half_view(at, other, side, h):
        return full.at[
            pl.ds(pl.multiple_of(at * block, block), block),
            pl.ds(pl.multiple_of(h * half + side * cols + other * lanes, lanes), lanes)]

    def n_copy(k, other):
        h, m = k // each, k % each
        return pltpu.make_async_remote_copy(
            nbuf.at[k], half_view(p, xh, c, h), n_s.at[k, other], n_r.at[h, p, xh],
            device_id=(m * NZ + z, other * 2 + c), device_id_type=MESH)

    def n_local(k):
        h = k // each
        return pltpu.make_async_copy(nbuf.at[k], half_view(p, xh, c, h), n_r.at[h, p, xh])

    def n_mine(k, other):
        return jnp.logical_and(k % each == p, xh == other)

    def multiply(k):
        for d in range(1, NZ):
            slot = (z + d) % NZ
            landed(og_view(slot, k), og_r.at[k, slot])
        step = 2 * block
        for r in range(ny):
            acc = jnp.dot(xall[r * step:(r + 1) * step, :], ogs[k], preferred_element_type=F32)
            part[k, 0, r] = acc[:block].astype(BF16)
            part[k, 1, r] = acc[block:].astype(BF16)

    def middle_x(k):
        landed(sums.at[k, pl.ds(0, ny)], rs_r.at[k, ny])
        for d in (2, 1, 3, 0):
            to = (y + d) % ny
            total = part[k, xl, to].astype(F32) + sums[k, to].astype(F32)
            if d:
                mids[k, to] = total.astype(BF16)
                x_then_y_second(k, d).start()
            else:
                kept[k] = total

    def middle_y(k):
        mine = part[k, xl, y].astype(F32)
        other = part[k, 1 - xl, y].astype(F32)
        for d in range(1, ny):
            source = (y + d) % ny
            landed(sums.at[k, pl.ds(2 * source, 2)], rs_r.at[k, source])
            mine = mine + sums[k, 2 * source + xl].astype(F32)
            other = other + sums[k, 2 * source + 1 - xl].astype(F32)
        mids[k, 0] = other.astype(BF16)
        y_then_x_second(k).start()
        kept[k] = mine

    def combine_x(k):
        total = kept[k]
        for d in range(1, ny):
            source = (y + d) % ny
            landed(sums.at[k, ny + source], rs_r.at[k, source])
            total = total + sums[k, ny + source].astype(F32)
        combine(k, total)

    def combine_y(k):
        landed(sums.at[k, 2 * y], rs_r.at[k, ny])
        combine(k, kept[k] + sums[k, 2 * y].astype(F32))

    def mom_landed(h):
        for d in range(1, NZ):
            slot = (z + d) % NZ
            landed(moms.at[slot, pl.ds(h * each, each)], mo_r.at[h, slot])

    def combine(k, total):
        momentum = moms[:, k].reshape(block, lanes).astype(F32)
        gbuf[k] = total.astype(BF16)
        nbuf[k] = (total + 0.95 * (0.95 * momentum + total)).astype(BF16)
        for other in range(2):
            mine = n_mine(k, other)

            @pl.when(jnp.logical_not(mine))
            def _():
                n_copy(k, other).start()

            @pl.when(mine)
            def _():
                n_local(k).start()

    def n_forward(h, at, other):
        view = half_view(at, other, c, h)
        return pltpu.make_async_remote_copy(
            view, view, nf_s.at[h, at, other], nf_r.at[h, at, other],
            device_id=(fs, partner), device_id_type=MESH)

    def forward_half(h):
        @pl.loop(0, planes)
        def _(step):
            at = (p + step) % planes
            for other in range(2):
                landed(half_view(at, other, c, h), n_r.at[h, at, other])
                n_forward(h, at, other).start()

    def take_half(h):
        @pl.loop(0, planes)
        def _(step):
            at = (p + step) % planes
            for other in range(2):
                landed(half_view(at, other, 1 - c, h), nf_r.at[h, at, other])

    matrix = z * each + p
    tile = 256
    homes = tile // piece

    def back_copy(to):
        return pltpu.make_async_remote_copy(
            final.at[pl.ds(pl.multiple_of(to * piece, piece), piece), :], back.at[matrix], b_s.at[to],
            b_r.at[matrix], device_id=(to, t), device_id_type=MESH)

    def outer(ref, here, span):
        return lax.dot_general(
            ref[here, span], ref[:, span], (((1,), (1,)), ((), ())), preferred_element_type=F32)

    def square_sum(low, high):
        acc = jnp.zeros((tile, high - low), F32)
        for r in range(0, rows, tile):
            value = full[r:r + tile, low:high].astype(F32)
            acc = acc + value * value
        return jnp.sum(acc)

    def tiles(body):
        @pl.loop(0, rows, step=tile)
        def _(r):
            body(pl.ds(pl.multiple_of(r, tile), tile))

    def first_half():
        def body(here):
            wide[here, :] = outer(full, here, slice(0, half))

        tiles(body)
        squares[0] = square_sum(0, half)

    def mixers():
        def body(here):
            square = jnp.dot(gram[here, :], gram[...], preferred_element_type=F32)
            mix[here, :] = (-4.775 * gram[here, :].astype(F32) + 2.0315 * square).astype(BF16)

        tiles(body)

    def second_half():
        own = pl.ds(pl.multiple_of(half + c * cols, cols), cols)
        rest = pl.ds(pl.multiple_of(half + (1 - c) * cols, cols), cols)

        def with_own(here):
            wide[here, :] = wide[here, :] + outer(full, here, own)

        tiles(with_own)
        take_half(1)
        inverse = 1.0 / (jnp.sqrt(squares[0] + square_sum(half, rows)) + 1e-07)

        def with_rest(here):
            gram[here, :] = ((wide[here, :] + outer(full, here, rest)) * inverse * inverse).astype(BF16)

        tiles(with_rest)
        mixers()

        def advance(here):
            product = jnp.dot(mix[here, :], full[...], preferred_element_type=F32)
            xs[here, :] = ((3.4445 * full[here, :].astype(F32) + product) * inverse).astype(BF16)

        tiles(advance)

        def again(here):
            gram[here, :] = outer(xs, here, slice(None)).astype(BF16)

        tiles(again)
        mixers()
        for h in range(2):
            thin[:, h * lanes:(h + 1) * lanes] = xs[:, pl.ds(
                pl.multiple_of(h * half + c * cols + xh * lanes, lanes), lanes)]

        @pl.loop(0, rows // tile)
        def _(i):
            at = (i + p) % (rows // tile)
            here = pl.ds(pl.multiple_of(at * tile, tile), tile)
            product = jnp.dot(mix[here, :], thin[...], preferred_element_type=F32)
            final[here, :] = (3.4445 * thin[here, :].astype(F32) + product).astype(BF16)

            @pl.loop(0, homes)
            def _(step):
                to = at * homes + (step + z) % homes

                @pl.when(to != fs)
                def _():
                    back_copy(to).start()

        pltpu.make_async_copy(
            final.at[pl.ds(pl.multiple_of(fs * piece, piece), piece), :], back.at[matrix], b_r.at[matrix]).start()

    def home_copy(d):
        to = (z + d) % NZ
        return pltpu.make_async_remote_copy(
            gbuf.at[:, pl.ds(pl.multiple_of(to * piece, piece), piece), :], home.at[pl.ds(z * chunks, chunks)],
            h_s.at[d], h_r.at[z], device_id=(p * NZ + to, t), device_id_type=MESH)

    owner = p < each

    @pl.loop(0, each)
    def _(j):
        k = 2 * j
        multiply(k)
        x_then_y_first(k).start()

        @pl.when(j >= 1)
        def _():
            middle_x(k - 2)

        @pl.when(j == 2)
        def _():
            mom_landed(0)

        late = jnp.logical_and(j >= 2, j < 2 + each // 2)

        @pl.when(late)
        def _():
            combine_x(k - 4)

        multiply(k + 1)
        for d in (2, 1, 3):
            y_then_x_first(k + 1, d).start()

        @pl.when(j >= 1)
        def _():
            middle_y(k - 1)

        @pl.when(late)
        def _():
            combine_y(k - 3)

    middle_x(chunks - 2)

    @pl.when(owner)
    def _():
        forward_half(0)
        take_half(0)
        first_half()

    middle_y(chunks - 1)
    mom_landed(1)

    @pl.loop(each // 2, each)
    def _(j):
        combine_x(2 * j)
        combine_y(2 * j + 1)

    for d in range(1, NZ):
        home_copy(d).start()
    own_home = pltpu.make_async_copy(
        gbuf.at[:, pl.ds(pl.multiple_of(z * piece, piece), piece), :], home.at[pl.ds(z * chunks, chunks)], loc.at[3])
    own_home.start()

    @pl.when(owner)
    def _():
        forward_half(1)
        second_half()

    own_home.wait()
    for d in range(1, NZ):
        slot = (z + d) % NZ
        landed(home.at[pl.ds(slot * chunks, chunks)], h_r.at[slot])

    @pl.loop(0, groups)
    def _(source):
        sp, sz = source // NZ, source % NZ

        @pl.when(sp < each)
        def _():
            landed(back.at[sz * each + sp], b_r.at[sz * each + sp])

    @pl.when(owner)
    def _():
        for h in range(2):
            @pl.loop(0, planes)
            def _(at):
                for other in range(2):
                    n_forward(h, at, other).wait_send()

        @pl.loop(1, groups)
        def _(d):
            back_copy((fs + d) % groups).wait_send()

    for d in range(1, NZ):
        x_copy(d).wait_send()
        x_forward((z + d) % NZ).wait_send()
        home_copy(d).wait_send()
        for h in range(2):
            mom_copy(d, h).wait_send()

    @pl.loop(0, each)
    def _(j):
        x_then_y_first(2 * j).wait_send()
        y_then_x_second(2 * j + 1).wait_send()
        for d in range(1, ny):
            x_then_y_second(2 * j, d).wait_send()
            y_then_x_first(2 * j + 1, d).wait_send()

    @pl.loop(0, chunks)
    def _(k):
        for d in range(1, NZ):
            og_copy(d, k).wait_send()
        for other in range(2):
            @pl.when(jnp.logical_not(n_mine(k, other)))
            def _():
                n_copy(k, other).wait_send()


def finish_kernel(each, rows, home, back, momentum_ref, new_ref, update_ref):
    count, piece, cols = back.shape
    lanes = cols // 2
    for base in range(0, count, 8):
        group = slice(base, base + 8)
        update_ref[:, group, :] = jnp.swapaxes(back[group].astype(F32), 0, 1) * (0.2 * math.sqrt(rows))
        for h in range(2):
            here = slice(h * lanes, (h + 1) * lanes)
            grads = jnp.stack([home[m // each * 2 * each + h * each + m % each] for m in range(base, base + 8)])
            new_ref[:, group, here] = 0.95 * momentum_ref[:, group, here] + jnp.swapaxes(grads.astype(F32), 0, 1)


def local(inputs, out_grads, momentum):
    groups = lax.axis_size("fsdp")
    planes = groups // NZ
    tok, count, cols = out_grads.shape
    rows = inputs.shape[1]
    piece = momentum.shape[0]
    each = count // NZ
    chunks = 2 * each
    lanes = cols // 2
    block = rows // planes
    dma = pltpu.SemaphoreType.DMA
    vmem = pl.BlockSpec(memory_space=pltpu.VMEM)
    hbm = pl.BlockSpec(memory_space=pl.ANY)
    home, back = pl.pallas_call(
        functools.partial(step_kernel, groups),
        out_shape=(
            jax.ShapeDtypeStruct((2 * count, piece, lanes), BF16), jax.ShapeDtypeStruct((count, piece, cols), BF16)),
        in_specs=[vmem, hbm, hbm],
        out_specs=(hbm, hbm),
        scratch_shapes=[
            pltpu.VMEM((rows, tok), BF16),
            pltpu.VMEM((2 * count, tok, lanes), BF16),
            pltpu.VMEM((2 * count, piece, lanes), BF16),
            pltpu.VMEM((tok, count, cols), BF16),
            pltpu.VMEM((piece, count, cols), F32),
            pltpu.VMEM((rows, NZ * tok), BF16),
            pltpu.VMEM((chunks, NZ * tok, lanes), BF16),
            pltpu.VMEM((NZ, chunks, piece, lanes), BF16),
            pltpu.VMEM((chunks, 2, planes // 2, block, lanes), BF16),
            pltpu.VMEM((chunks, planes, block, lanes), BF16),
            pltpu.VMEM((chunks, planes // 2, block, lanes), BF16),
            pltpu.VMEM((chunks, block, lanes), F32),
            pltpu.VMEM((chunks, block, lanes), BF16),
            pltpu.VMEM((chunks, block, lanes), BF16),
            pltpu.VMEM((rows, rows), BF16),
            pltpu.VMEM((rows, rows), F32),
            pltpu.VMEM((rows, rows), BF16),
            pltpu.VMEM((rows, rows), BF16),
            pltpu.VMEM((rows, rows), BF16),
            pltpu.VMEM((rows, cols), BF16),
            pltpu.VMEM((rows, cols), BF16),
            pltpu.SMEM((1,), F32),
            dma((NZ,)), dma((NZ,)), dma((NZ,)), dma((NZ,)),
            dma((chunks, NZ)), dma((chunks, NZ)), dma((2, NZ)), dma((2, NZ)),
            dma((chunks, planes // 2)), dma((chunks, planes // 2 + 1)),
            dma((chunks, 2)), dma((2, planes, 2)), dma((2, planes, 2)), dma((2, planes, 2)),
            dma((NZ,)), dma((NZ,)), dma((groups,)), dma((count,)), dma((6,)),
        ],
        compiler_params=pltpu.CompilerParams(
            collective_id=0, has_side_effects=True, vmem_limit_bytes=60 * 1024 * 1024),
        name="muon_step",
    )(inputs, out_grads, momentum)
    return pl.pallas_call(
        functools.partial(finish_kernel, each, rows),
        out_shape=(jax.ShapeDtypeStruct(momentum.shape, F32), jax.ShapeDtypeStruct(momentum.shape, F32)),
        in_specs=[vmem, vmem, vmem],
        out_specs=(vmem, vmem),
        name="finish",
    )(home, back, momentum)


def solution(mesh):
    in_specs = (P("fsdp", None), P("fsdp", None, "tp"), P("fsdp", None, "tp"))
    out_specs = (P("fsdp", None, "tp"), P("fsdp", None, "tp"))
    return jax.shard_map(local, mesh=mesh, in_specs=in_specs, out_specs=out_specs, check_vma=False)
```

time: 125 us -> 114 us (0.912)
  Pallas kernels: 124 us -> 113 us
    pallas_call x1, Pallas kernels: 121 us -> 110 us  [local(): pl.pallas_call(functools.partial(step_kernel, groups), out_shape=(jax.Sha...]
where the time goes in v3:
time: 114 us; the launch traced here: 113 us
  Pallas kernels  113 us (99%)
    pallas_call x1, Pallas kernels, local(): pl.pallas_call(functools.partial(step_kernel, groups), out_shape=(jax.Sha...  110 us
    pallas_call x1, Pallas kernels, local(): pl.pallas_call(functools.partial(finish_kernel, each, rows), out_shape=(j...  2.83 us

profile of v3, /device:TPU:0, one launch (start us, length us, event | category | flops | bytes accessed | tf_op | source)
XLA Modules:
  0.0 113.4 jit_solution(7811620805606714780)
XLA Ops:
  0.6 109.9 %muon_step.1 = (bf16[48,32,128]{2,1,0:T(8,128)(2,1)}, bf16[24,32,256]{2,1,0:T(8,128)(2,1)}) custom-call(bf16[256,1024]{1,0:T(8,128)(2,1)} %x_ref.1, bf16[256,24,256]{2,1,0:T(8,128)(2,1)} %grads_ref.1, f32[32,24,256]{2,1,0:T(8,128)} %momentum_ref.3), custom_call_target="tpu_custom_call" | custom-call | tf_op jit(solution)/shard_map/muon_step/pallas_call | solution.py:504
  110.6 2.8 %finish.1 = (f32[32,24,256]{2,1,0:T(8,128)}, f32[32,24,256]{2,1,0:T(8,128)}) custom-call(bf16[48,32,128]{2,1,0:T(8,128)(2,1)} %get-tuple-element.4.home, bf16[24,32,256]{2,1,0:T(8,128)(2,1)} %get-tuple-element.5.back, f32[32,24,256]{2,1,0:T(8,128)} %momentum_ref.3), custom_call_target="tpu_custom_call" | custom-call | tf_op jit(solution)/shard_map/finish/pallas_call | solution.py:543
